TPU v7x, 128 devices: a whole 4x4x4 slice. The times are simulated.
128 devices in a mesh: outer: 8 (over z_lo, y), inner: 16 (over z_hi, x, core).
Axes of the slice: x: 4, y: 4, z: 4 (z_hi: 2, z_lo: 2; z = z_hi * 2 + z_lo), core: 2. Of those that a mesh axis runs over, the one named last changes fastest.
Arguments:
- tokens: bfloat16 [1024, 8192], P(None, 'outer'), may hold values from -60 to 60
- base_gate: bfloat16 [8192, 28672], P('outer', 'inner'), may hold values from -0.06629126 to 0.06629126
- base_up: bfloat16 [8192, 28672], P('outer', 'inner'), may hold values from -0.06629126 to 0.06629126
- adjusted_gate: bfloat16 [8192, 28672], P('outer', 'inner'), may hold values from -0.092807765 to 0.092807765
- adjusted_up: bfloat16 [8192, 28672], P('outer', 'inner'), may hold values from -0.092807765 to 0.092807765
- slab_block: int32 [16], replicated, may hold values from 0 to 15, each once
Outputs:
- correlation: float32 [1792, 28672], P('outer', 'inner')
Inputs may be any that keep to these rules, and one draw needn't show every extreme that they name: `slab_block`: each block number appears once.
All inputs are finite; a program needn't handle non-finite values.
Results may differ from a plain program's by a relative error of at most 0.004.
Values may be sent and summed in bfloat16 or wider, within the bound.
No kernel may reach another device: no remote copies, remote signals or barrier semaphores. Data moves between devices by JAX's collectives and lax.ppermute only.
A program may use at most 192 MiB of HBM per device.

v0:
```python
import jax
import jax.numpy as jnp
from jax import lax
from jax.sharding import PartitionSpec as P


def from_everyone(array, axis):
    count = lax.axis_size(axis)
    return lax.all_to_all(
        jnp.broadcast_to(array[None], (count, *array.shape)), axis, 0, 0, tiled=True
    )


def taken_together(array, axis):
    everything = from_everyone(array, axis)
    return jnp.sum(everything, axis=0)


def together(arrays, axis):
    ends = [0]
    for a in arrays:
        ends.append(ends[-1] + a.size)
    so_far = taken_together(jnp.concatenate([a.ravel() for a in arrays]), axis)
    return tuple((so_far[b:e].reshape(a.shape) for a, b, e in zip(arrays, ends, ends[1:])))


def picked(array, axis, root):
    return lax.dynamic_index_in_dim(lax.all_gather(array, axis), root, 0, keepdims=False)


def sent_together(arrays, axis, dim, along):
    both = jnp.concatenate(arrays, axis=along)
    filled, at, done = (lax.all_gather(both, axis, axis=dim, tiled=True), 0, [])
    for a in arrays:
        done.append(lax.slice_in_dim(filled, at, at + a.shape[along], axis=along))
        at += a.shape[along]
    return tuple(done)


def local(tokens, base_gate, base_up, adjusted_gate, adjusted_up, slab_block):
    units = base_gate.shape[1]
    total_tokens = tokens.shape[0]
    outer_count = lax.axis_size("outer")
    parts = [
        jnp.dot(tokens, weight, preferred_element_type=jnp.float32)
        for weight in (base_gate, base_up, adjusted_gate, adjusted_up)
    ]
    terms = lax.psum_scatter(
        jnp.concatenate(parts, axis=1), "outer", scatter_dimension=0, tiled=True
    )
    hidden_base = jax.nn.silu(terms[:, :units]) * terms[:, units : 2 * units]
    hidden_adjusted = jax.nn.silu(terms[:, 2 * units : 3 * units]) * terms[:, 3 * units :]
    hidden = jnp.concatenate([hidden_base, hidden_adjusted], axis=1)
    sums, squares = together(
        (jnp.sum(hidden, axis=0, keepdims=True), jnp.sum(hidden * hidden, axis=0, keepdims=True)),
        "outer",
    )
    mean = sums / total_tokens
    var = squares / total_tokens - mean * mean
    centered = hidden - mean
    standard = (centered * lax.rsqrt(var + 1e-05)).astype(jnp.bfloat16)
    base_scores = standard[:, :units]
    adjusted_scores = standard[:, units:]
    slab = picked(base_scores, "inner", slab_block[0])
    contract = (((0,), (0,)), ((), ()))
    full_slab, full_adjusted = sent_together((slab, adjusted_scores), "outer", 0, 1)
    row_count = units // outer_count
    own_rows = lax.dynamic_slice_in_dim(
        full_slab, lax.axis_index("outer") * row_count, row_count, 1
    )
    gram = lax.dot_general(own_rows, full_adjusted, contract, preferred_element_type=jnp.float32)
    return gram / total_tokens


def solution(mesh):
    return jax.shard_map(
        local,
        mesh=mesh,
        in_specs=(
            P(None, "outer"),
            P("outer", "inner"),
            P("outer", "inner"),
            P("outer", "inner"),
            P("outer", "inner"),
            P(),
        ),
        out_specs=P("outer", "inner"),
        check_vma=False,
    )
```

profile of v0, /device:TPU:1, one launch (start us, length us, event | category | flops | bytes accessed | tf_op | source)
XLA Modules:
  0.0 524.5 jit_solution(9301898634528933098)
XLA Ops:
  6.5 0.0 copy-start
  6.5 0.0 reduce-scatter.2.cloned.1.call-start
  6.5 1.6 copy-done
  8.1 0.0 copy-start.3
  8.1 8.1 %fusion.12 = f32[1024,1792]{1,0:T(8,128)} fusion(bf16[1024,1024]{1,0:T(8,128)(2,1)S(1)} %copy-done, bf16[1024,1792]{1,0:T(8,128)(2,1)} %param.7), kind=kOutput, calls=%fused_computation.21 | convolution fusion | flops 3758096384 | bytes 13107200 | tf_op jit(solution)/shard_map/dot_general | solution.py:45
  16.3 0.0 copy-done.3
  16.3 0.0 copy-start.4
  16.3 5.9 %fusion.13 = f32[1024,1792]{1,0:T(8,128)} fusion(bf16[1024,1024]{1,0:T(8,128)(2,1)S(1)} %copy-done, bf16[1024,1792]{1,0:T(8,128)(2,1)S(1)} %copy-done.3), kind=kOutput, calls=%fused_computation.22 | convolution fusion | flops 3758096384 | bytes 13107200 | tf_op jit(solution)/shard_map/dot_general | solution.py:45
  22.2 0.0 copy-done.4
  22.2 0.0 copy-start.5
  22.2 6.0 %fusion.14 = f32[1024,1792]{1,0:T(8,128)} fusion(bf16[1024,1024]{1,0:T(8,128)(2,1)S(1)} %copy-done, bf16[1024,1792]{1,0:T(8,128)(2,1)S(1)} %copy-done.4), kind=kOutput, calls=%fused_computation.23 | convolution fusion | flops 3758096384 | bytes 13107200 | tf_op jit(solution)/shard_map/dot_general | solution.py:45
  28.2 0.0 copy-done.5
  28.2 5.9 %fusion.15 = f32[1024,1792]{1,0:T(8,128)} fusion(bf16[1024,1024]{1,0:T(8,128)(2,1)S(1)} %copy-done, bf16[1024,1792]{1,0:T(8,128)(2,1)S(1)} %copy-done.5), kind=kOutput, calls=%fused_computation.24 | convolution fusion | flops 3758096384 | bytes 13107200 | tf_op jit(solution)/shard_map/dot_general | solution.py:45
  34.1 20.9 %pad_maximum_fusion = f32[1024,7168]{1,0:T(8,128)} fusion(f32[1024,1792]{1,0:T(8,128)} %fusion.15, f32[1024,1792]{1,0:T(8,128)} %fusion.14, f32[1024,1792]{1,0:T(8,128)} %fusion.13, f32[1024,1792]{1,0:T(8,128)} %fusion.12), kind=kLoop, calls=%fused_computation | loop fusion | flops 22020096 | bytes 58720256 | tf_op jit(solution)/shard_map/concatenate | solution.py:49
  55.0 0.0 reduce-scatter.2.cloned.1.call-update
  55.1 0.0 all-gather.6.cloned.1.call-start
  55.1 293.1 %reduce-scatter.2.cloned.1.call-done = f32[128,7168]{1,0:T(8,128)} async-done(((f32[1024,7168]{1,0:T(8,128)}), f32[128,7168]{1,0:T(8,128)}) %reduce-scatter.2.cloned.1.call-update) | async-done | bytes 3670032 | tf_op jit(solution)/shard_map/reduce_scatter | solution.py:48
  348.2 2.5 slice_multiply_fusion.1
  350.7 0.0 copy-start.2
  350.7 0.2 fusion.5
  350.9 0.1 broadcast_in_dim.2
  351.0 8.5 %all_to_all.6 = f32[8,1,7168]{2,1,0:T(1,128)S(1)} all-to-all(f32[8,1,7168]{2,1,0:T(1,128)S(1)} %broadcast_in_dim.2), channel_id=1, replica_groups=mesh['outer'=8,'inner'=16] {'outer'}, dimensions={0} | all-to-all | bytes 458752 | tf_op jit(solution)/shard_map/all_to_all | solution.py:9
  359.5 0.2 reduce_sum.29
  359.7 0.2 multiply_convert_fusion
  359.9 0.8 fusion.11
  360.7 0.0 all-gather.6.cloned.1.call-update
  360.7 0.0 all-gather.4.cloned.1.call-start
  360.8 0.0 copy-done.2
  360.9 69.1 %all-gather.6.cloned.1.call-done = bf16[2048,1792]{1,0:T(8,128)(2,1)} async-done(((bf16[128,1792]{1,0:T(8,128)(2,1)}), bf16[2048,1792]{1,0:T(8,128)(2,1)}) %all-gather.6.cloned.1.call-update) | async-done | bytes 7340048 | tf_op jit(solution)/shard_map/all_gather | solution.py:28
  430.0 1.0 dynamic-slice_bitcast_fusion
  431.1 1.0 pad_maximum_fusion.2
  432.1 0.0 all-gather.4.cloned.1.call-update
  432.1 79.5 %all-gather.4.cloned.1.call-done = bf16[1024,3584]{1,0:T(8,128)(2,1)} async-done(((bf16[128,3584]{1,0:T(8,128)(2,1)}), bf16[1024,3584]{1,0:T(8,128)(2,1)}) %all-gather.4.cloned.1.call-update) | async-done | bytes 7340048 | tf_op jit(solution)/shard_map/all_gather | solution.py:33
  511.6 0.0 slice-start
  511.6 0.0 copy-start.1
  511.6 2.0 slice-done
  513.6 4.3 fusion.2
  517.9 0.0 copy-done.1
  (2 shorter events, 0.0 us)
Async XLA Ops:
  6.5 1.6 copy-start
  6.5 341.6 %reduce-scatter.2.cloned.1.call-start = ((), (), s32[]{:S(2)}) async-start(), calls=%async_computation.2 | async-start | bytes 33030144 | tf_op jit(solution)/shard_map/reduce_scatter | solution.py:48
  8.1 8.1 %copy-start.3 = (bf16[1024,1792]{1,0:T(8,128)(2,1)S(1)}, bf16[1024,1792]{1,0:T(8,128)(2,1)}, u32[]{:S(2)}) copy-start(bf16[1024,1792]{1,0:T(8,128)(2,1)} %param.8) | copy-start | bytes 11010052
  16.3 5.9 %copy-start.4 = (bf16[1024,1792]{1,0:T(8,128)(2,1)S(1)}, bf16[1024,1792]{1,0:T(8,128)(2,1)}, u32[]{:S(2)}) copy-start(bf16[1024,1792]{1,0:T(8,128)(2,1)} %param.9) | copy-start | bytes 11010052
  22.2 6.0 %copy-start.5 = (bf16[1024,1792]{1,0:T(8,128)(2,1)S(1)}, bf16[1024,1792]{1,0:T(8,128)(2,1)}, u32[]{:S(2)}) copy-start(bf16[1024,1792]{1,0:T(8,128)(2,1)} %param.10) | copy-start | bytes 11010052
  55.1 375.0 %all-gather.6.cloned.1.call-start = ((), (), s32[]{:S(2)}) async-start(), calls=%async_computation.4 | async-start | bytes 7798784 | tf_op jit(solution)/shard_map/all_gather | solution.py:28
  350.7 10.1 %copy-start.2 = (s32[16]{0:T(128)S(1)}, s32[16]{0:T(128)}, u32[]{:S(2)}) copy-start(s32[16]{0:T(128)} %param.11) | copy-start | bytes 196
  360.7 150.9 %all-gather.4.cloned.1.call-start = ((), (), s32[]{:S(2)}) async-start(), calls=%async_computation.3 | async-start | bytes 8257536 | tf_op jit(solution)/shard_map/all_gather | solution.py:33
  511.6 2.0 slice-start
  511.6 6.3 %copy-start.1 = (bf16[1024,1024]{1,0:T(8,128)(2,1)S(1)}, bf16[1024,1024]{1,0:T(8,128)(2,1)}, u32[]{:S(2)}) copy-start(bf16[1024,1024]{1,0:T(8,128)(2,1)} %param.6) | copy-start | bytes 6291460
Sparse Core Ops, SparseCore 0:
  55.2 292.9 reduce-scatter.1
  360.8 69.1 all-gather.5
  432.2 79.3 all-gather.3
where the time goes:
time: 525 us; the launch traced here: 524 us
  waiting for transfers between devices  442 us (84%)
  matrix products  30.3 us (6%)
  other arithmetic  25 us (5%)
  between operations  13.3 us (3%)
  blocking collectives  8.46 us (2%)
  local copies, waits for them, and re-layouts  5.64 us (1%)
    reduce_scatter x1, waiting for transfers between devices, local(): lax.psum_scatter(jnp.concatenate(parts, axis=1), 'outer', scatter_dimensi...  293 us
    all_gather x1, waiting for transfers between devices, sent_together(): filled, at, done = (lax.all_gather(both, axis, axis=dim, tiled=True), 0, [])  79.5 us
    all_gather x1, waiting for transfers between devices, picked(): lax.all_gather(array, axis)  69.1 us
    dot_general x4, matrix products, local(): jnp.dot(tokens, weight, preferred_element_type=jnp.float32)  26 us
    concatenate x1, other arithmetic, local(): jnp.concatenate(parts, axis=1)  20.9 us
  transfers between devices with their start and end apart: 3, of which 3 were waited for; matrix products, arithmetic and copies ran while one was open for 0% of the time, Pallas kernels for 0%

commit v1 on v0

v1 whole, which is shorter than its diff:
```python
import jax
import jax.numpy as jnp
from jax import lax
from jax.experimental import pallas as pl
from jax.experimental.pallas import tpu as pltpu
from jax.sharding import PartitionSpec as P

Y, Z, X = 4, 2, 4
TILE = 128
BLOCK = 16
BF = jnp.bfloat16
F32 = jnp.float32


def along_y(k):
    return [(z * Y + y, z * Y + (y + k) % Y) for z in range(Z) for y in range(Y)]


def across_z():
    return [(o, o ^ Y) for o in range(Z * Y)]


def along_x(k):
    return [(h * 8 + x * 2 + c, h * 8 + (x + k) % X * 2 + c) for h in range(2) for x in range(X) for c in range(2)]


def flip(bit):
    return [(i, i ^ bit) for i in range(16)]


def to_outer(array, perm):
    return lax.ppermute(array, "outer", perm)


def to_inner(array, perm):
    return lax.ppermute(array, "inner", perm)


def project(weight, tokens):
    return lax.dot_general(weight, tokens, (((0,), (1,)), ((), ())), preferred_element_type=F32)


def standardized(gate, up):
    hidden = jax.nn.silu(gate) * up
    mean = jnp.mean(hidden, axis=1, keepdims=True)
    centered = hidden - mean
    var = jnp.mean(centered * centered, axis=1, keepdims=True)
    return (centered * lax.rsqrt(var + 1e-05)).astype(BF)


def projected(weight, tokens, plan):
    depth, units = weight.shape
    count = tokens.shape[0]
    rows, wide = units // (Z * Y), 2 * TILE
    steps = units // wide

    def kernel(w_ref, t_ref, *refs):
        outs, total = refs[:-1], refs[-1]
        step = pl.program_id(0)
        at = pl.ds(pl.multiple_of(step * wide, wide), wide)
        total[at] = project(w_ref[...], t_ref[...])

        @pl.when(step == steps - 1)
        def _():
            outer = lax.axis_index("outer")
            y, z = outer % Y, outer // Y
            for n, place, dz, dy in plan["parts"]:
                row = pl.multiple_of(((z + dz) % Z * Y + (y + dy) % Y) * rows, BLOCK)
                part = total[pl.ds(row, rows)].astype(outs[n].dtype)
                if place is None:
                    outs[n][...] = part
                else:
                    outs[n][place] = part

    whole = lambda shape: pl.BlockSpec(shape, lambda i: (0,) * len(shape), pipeline_mode=pl.Buffered(1))
    shapes = [((*lead, rows, count), dtype) for lead, dtype in plan["shapes"]]
    return pl.pallas_call(
        kernel,
        grid=(steps,),
        in_specs=[pl.BlockSpec((depth, wide), lambda i: (0, i)), whole((count, depth))],
        out_specs=[whole(shape) for shape, _ in shapes],
        out_shape=[jax.ShapeDtypeStruct(shape, dtype) for shape, dtype in shapes],
        scratch_shapes=[pltpu.VMEM((units, count), F32)],
        compiler_params=pltpu.CompilerParams(vmem_limit_bytes=28 * 1024 * 1024),
        cost_estimate=pl.CostEstimate(flops=2 * depth * units * count, bytes_accessed=2 * depth * (units + count), transcendentals=0),
    )(in_hbm(weight), tokens)


STEPS_Y = (2, 1, 3)
GATE_PLAN = {
    "shapes": [((Z,), F32)] + [((Z,), BF)] * 3,
    "parts": [(n + 1, dz, dz, k) for n, k in enumerate(STEPS_Y) for dz in range(Z)] + [(0, dz, dz, 0) for dz in range(Z)],
}
UP_PLAN = {
    "shapes": [((Y,), F32)] + [((), BF)] * 4,
    "parts": [(n + 1, None, 1, k) for n, k in enumerate((2, 1, 3, 0))] + [(0, k, 0, k) for k in range(Y)],
}


def summed_y_first(weight, tokens):
    total, *parts = projected(weight, tokens, GATE_PLAN)
    came = [to_outer(part, along_y(k)) for k, part in zip(STEPS_Y, parts)]
    for c in came:
        total = total + c.astype(F32)
    narrow = total[1].astype(BF)
    other = to_outer(narrow, across_z())
    return total[0] + other.astype(F32)


def summed_z_first(weight, tokens):
    own, *parts = projected(weight, tokens, UP_PLAN)
    came = {k: to_outer(part, across_z()) for k, part in zip((2, 1, 3, 0), parts)}
    total, narrow = {}, {}
    for k in came:
        total[k] = own[k] + came[k].astype(F32)
        if k:
            narrow[k] = total[k].astype(BF)
            own, narrow[k] = lax.optimization_barrier((own, narrow[k]))
    result = total[0]
    for k in STEPS_Y:
        result = result + to_outer(narrow[k], along_y(k)).astype(F32)
    return result


def gathered(score):
    held = {0: score}
    for k in STEPS_Y:
        held[k] = to_outer(score, along_y(k))
    pieces = []
    for k in (0, *STEPS_Y):
        pieces += [(held[k], 0, k), (to_outer(held[k], across_z()), 1, k)]
    return pieces


def in_hbm(array):
    return pltpu.with_memory_space_constraint(array, pltpu.HBM)


def moved(kernel, shapes, n_copies, root, arrays):
    size = sum(2 * jnp.size(a) for a in (jax.eval_shape(lambda s=s: jnp.zeros(s, BF)) for s in shapes))
    return pl.pallas_call(
        kernel,
        in_specs=[pl.BlockSpec(memory_space=pltpu.SMEM)] + [pl.BlockSpec(memory_space=pl.ANY)] * len(arrays),
        out_specs=[pl.BlockSpec(memory_space=pltpu.VMEM)] * len(shapes),
        out_shape=[jax.ShapeDtypeStruct(s, BF) for s in shapes],
        scratch_shapes=[pltpu.SemaphoreType.DMA((n_copies,))],
        compiler_params=pltpu.CompilerParams(vmem_limit_bytes=16 * 1024 * 1024),
        cost_estimate=pl.CostEstimate(flops=0, bytes_accessed=2 * size, transcendentals=0),
    )(root[None], *arrays)


def halves(weights, root):
    depth, units = weights[0].shape
    half = units // 2

    def kernel(root_ref, *refs):
        ins, out, sems = refs[:2], refs[2], refs[3]
        at = pl.multiple_of((1 - lax.axis_index("inner") % 2) * half, TILE)
        copies = [pltpu.make_async_copy(ins[n].at[:, pl.ds(at, half)], out.at[n], sems.at[n]) for n in range(2)]
        for c in copies:
            c.start()
        for c in copies:
            c.wait()

    return moved(kernel, [(2, depth, half)], 2, root, weights)[0]


def chunks(weights, swapped, root):
    depth, units = weights[0].shape
    half, wide = units // 2, 2 * TILE

    def kernel(root_ref, *refs):
        ins, outs, sems = refs[:3], refs[3:-1], refs[-1]
        inner = lax.axis_index("inner")
        x, c = inner // 2 % X, inner % 2
        at_home = root_ref[0] % 2 == c
        copies = []
        for k in range(X):
            at = jnp.minimum((x + k) % X * wide, half - wide)
            for n in range(2):
                sem, out = sems.at[2 * k + n], outs[k].at[n]
                here = pltpu.make_async_copy(ins[n].at[:, pl.ds(pl.multiple_of(c * half + at, TILE), wide)], out, sem)
                there = pltpu.make_async_copy(ins[2].at[n, :, pl.ds(pl.multiple_of(at, TILE), wide)], out, sem)
                pl.when(at_home)(here.start)
                pl.when(jnp.logical_not(at_home))(there.start)
                copies.append(there)
        for made in copies:
            made.wait()

    return moved(kernel, [(2, depth, wide)] * X, 2 * X, root, (*weights, swapped))


def tiles(held, root):
    depth = held[0].shape[1]

    def kernel(root_ref, *refs):
        ins, outs, sems = refs[:X], refs[X:-1], refs[-1]
        inner = lax.axis_index("inner")
        h, x = inner // 8, inner // 2 % X
        away = (x + X - root_ref[0] // 2 % X) % X
        copies = []
        for n, which in enumerate((h, 1 - h)):
            for k in range(X):
                at = pl.ds(pl.multiple_of(which * TILE, TILE), TILE)
                made = pltpu.make_async_copy(ins[k].at[:, :, at], outs[n], sems.at[n])
                pl.when(away == k)(made.start)
            copies.append(made)
        for made in copies:
            made.wait()

    return moved(kernel, [(2, depth, TILE)] * 2, 2, root, held)


def slab_partials(mine, other, tokens, root):
    depth, count = mine.shape[1], tokens.shape[0]

    def kernel(root_ref, mine_ref, other_ref, t_ref, *refs):
        outs, total = refs[:-1], refs[-1]
        outer = lax.axis_index("outer")
        y, z = outer % Y, outer // Y
        at_home = root_ref[0] // 8 == lax.axis_index("inner") // 8
        for n in range(2):

            @pl.when(at_home)
            def _():
                total[n] = project(mine_ref[n], t_ref[...])

            @pl.when(jnp.logical_not(at_home))
            def _():
                total[n] = project(other_ref[n], t_ref[...])

            for k in range(Y):
                for dz in range(Z):
                    row = ((z + dz) % Z * Y + (y + k) % Y) * BLOCK
                    outs[k][n, dz] = total[n, pl.ds(pl.multiple_of(row, BLOCK), BLOCK)]

    vmem = pl.BlockSpec(memory_space=pltpu.VMEM)
    return pl.pallas_call(
        kernel,
        in_specs=[pl.BlockSpec(memory_space=pltpu.SMEM)] + [vmem] * 3,
        out_specs=[vmem] * Y,
        out_shape=[jax.ShapeDtypeStruct((2, Z, BLOCK, count), F32)] * Y,
        scratch_shapes=[pltpu.VMEM((2, TILE, count), F32)],
        compiler_params=pltpu.CompilerParams(vmem_limit_bytes=16 * 1024 * 1024),
        cost_estimate=pl.CostEstimate(flops=4 * depth * TILE * count, bytes_accessed=4 * count * depth, transcendentals=0),
    )(root[None], mine, other, tokens)


def spread(weights, tokens, root):
    weights = [in_hbm(w) for w in weights]
    half = halves(weights, root)
    swapped = to_inner(half, flip(1))
    chunk = chunks(weights, swapped, root)
    held = [chunk[0]] + [to_inner(chunk[k], along_x(k)) for k in (1, 2, 3)]
    mine, other = tiles(held, root)
    other = to_inner(other, flip(8))
    return slab_partials(mine, other, tokens, root)


def slab_moves():
    moves = []
    for i in range(16):
        h, x, c = i // 8, i // 2 % X, i % 2
        tile = min(2 * x, 5) + h
        if x == 3 and h == 0:
            continue
        for o in range(Z * Y):
            unit = 8 * (7 * c + tile) + o
            moves.append((o * 16 + i, unit // 14 * 16 + unit % 14))
    return moves


def correlate(pieces, blocks, rows, count):
    n_units = Z * Y * rows
    wide = 2 * TILE
    order = (0, 1, 8, 9)

    def kernel(*refs):
        ins, out, slab, scores, sems = refs[:-4], refs[-4], refs[-3], refs[-2], refs[-1]
        outer, inner = lax.axis_index("outer"), lax.axis_index("inner")
        z, y = outer // Y, outer % Y
        h, x, c = inner // 8, inner // 2 % X, inner % 2
        copies = []

        def copy(src, dst):
            made = pltpu.make_async_copy(src, dst, sems.at[len(copies)])
            made.start()
            copies.append(made)

        for ref, (_, dz, dy) in zip(ins, pieces):
            row = ((z + dz) % Z * Y + (y + Y - dy) % Y) * rows
            copy(ref, scores.at[pl.ds(pl.multiple_of(row, BLOCK), rows)])
        for ref, (block, dx) in zip(ins[len(pieces) :], blocks):
            for n, bits in enumerate(order):
                to_h, to_c = (h + bits // 8) % 2, (c + bits % 2) % 2
                slot = to_h * 8 + (x + X - dx) % X * 2 + to_c
                copy(ref.at[n], slab.at[pl.ds(pl.multiple_of(slot * BLOCK, BLOCK), BLOCK)])
        for made in copies:
            made.wait()
        left = slab[:rows]
        for n in range(n_units // wide):
            right = scores[n * wide : (n + 1) * wide]
            gram = lax.dot_general(left, right, (((1,), (1,)), ((), ())), preferred_element_type=F32)
            out[:, n * wide : (n + 1) * wide] = gram / count

    arrays = [p[0] for p in pieces] + [b[0] for b in blocks]
    n_copies = sum(a.shape[0] if a.ndim == 3 else 1 for a in arrays)
    return pl.pallas_call(
        kernel,
        out_shape=jax.ShapeDtypeStruct((rows, n_units), F32),
        in_specs=[pl.BlockSpec(memory_space=pl.ANY)] * len(arrays),
        out_specs=pl.BlockSpec(memory_space=pltpu.VMEM),
        scratch_shapes=[
            pltpu.VMEM((16 * BLOCK, count), BF),
            pltpu.VMEM((n_units, count), BF),
            pltpu.SemaphoreType.DMA((n_copies,)),
        ],
        compiler_params=pltpu.CompilerParams(vmem_limit_bytes=24 * 1024 * 1024),
        cost_estimate=pl.CostEstimate(
            flops=2 * rows * n_units * count, bytes_accessed=2 * (rows + n_units) * count + 4 * rows * n_units, transcendentals=0
        ),
    )(*arrays)


def local(tokens, base_gate, base_up, adjusted_gate, adjusted_up, slab_block):
    units = base_gate.shape[1]
    count = tokens.shape[0]
    rows = units // (Z * Y)
    root = slab_block[0]
    total, *parts = spread((base_gate, base_up), tokens, root)
    gate = summed_y_first(adjusted_gate, tokens)
    up = summed_z_first(adjusted_up, tokens)
    pieces = gathered(standardized(gate, up))

    for k, part in zip((1, 2, 3), parts):
        total = total + to_outer(part, along_y(k))
    total = total[:, 0] + to_outer(total[:, 1], across_z())
    score = standardized(total[0], total[1])
    score = lax.ppermute(score, ("outer", "inner"), slab_moves())
    two = jnp.stack([score, to_inner(score, flip(1))])
    four = jnp.concatenate([two, to_inner(two, flip(8))])
    blocks = [(four, 0)] + [(to_inner(four, along_x(k)), k) for k in (2, 1, 3)]
    return correlate(pieces, blocks, rows, count)


def solution(mesh):
    return jax.shard_map(
        local,
        mesh=mesh,
        in_specs=(
            P(None, "outer"),
            P("outer", "inner"),
            P("outer", "inner"),
            P("outer", "inner"),
            P("outer", "inner"),
            P(),
        ),
        out_specs=P("outer", "inner"),
        check_vma=False,
    )
```

time: 525 us -> 210 us (0.40)
  waiting for transfers between devices: 442 us -> 122 us
  starting transfers between devices: 0.09 us -> 55.9 us
  matrix products: 30.3 us -> 0 us
  Pallas kernels: 0 us -> 26 us
  other arithmetic: 25 us -> 2.55 us
  between operations: 13.3 us -> 0.42 us
  blocking collectives: 8.46 us -> 0 us
    reduce_scatter x1 -> x0, waiting for transfers between devices: 293 us -> none  [local(): lax.psum_scatter(jnp.concatenate(parts, axis=1), 'outer', scatter_dimensi...]
    all_gather x2 -> x0, waiting for transfers between devices: 149 us -> none  [the longest x1 79.5 us: sent_together(): filled, at, done = (lax.all_gather(both, axis, axis=dim, tiled=True), 0, [])]
    ppermute x0 -> x33, waiting for transfers between devices: none -> 122 us  [the longest x10 75.3 us: to_inner(): return lax.ppermute(array, 'inner', perm)]
    ppermute x0 -> x33, starting transfers between devices: none -> 55.9 us  [the longest x22 24.2 us: to_outer(): return lax.ppermute(array, 'outer', perm)]
    dot_general x5 -> x0, matrix products: 30.3 us -> none  [the longest x4 26 us: local(): jnp.dot(tokens, weight, preferred_element_type=jnp.float32)]
    pallas_call x0 -> x7, Pallas kernels: none -> 26 us  [the longest x2 15.2 us: projected(): pl.pallas_call(kernel, grid=(steps,), in_specs=[pl.BlockSpec((depth, wide...]
    concatenate x3 -> x1, other arithmetic: 21.9 us -> 0.02 us  [local(): four = jnp.concatenate([two, to_inner(two, flip(8))])]
    all_to_all x1 -> x0, blocking collectives: 8.46 us -> none  [from_everyone(): lax.all_to_all(jnp.broadcast_to(array[None], (count, *array.shape)), axis...]
  transfers between devices with their start and end apart: 3 -> 33, of which waited for: 3 -> 18; matrix products, arithmetic and copies ran while one was open for 0% -> 1% of each run, Pallas kernels for 0% -> 8%
where the time goes in v1:
time: 210 us; the launch traced here: 207 us
  waiting for transfers between devices  122 us (58%)
  starting transfers between devices  55.9 us (27%)
  Pallas kernels  26 us (12%)
  other arithmetic  2.55 us (1%)
    ppermute x10, waiting for transfers between devices, to_inner(): return lax.ppermute(array, 'inner', perm)  75.3 us
    ppermute x22, waiting for transfers between devices, to_outer(): return lax.ppermute(array, 'outer', perm)  43 us
    ppermute x22, starting transfers between devices, to_outer(): return lax.ppermute(array, 'outer', perm)  24.2 us
    ppermute x10, starting transfers between devices, to_inner(): return lax.ppermute(array, 'inner', perm)  22.1 us
    pallas_call x2, Pallas kernels, projected(): pl.pallas_call(kernel, grid=(steps,), in_specs=[pl.BlockSpec((depth, wide...  15.2 us
    ppermute x1, starting transfers between devices, local(): score = lax.ppermute(score, ('outer', 'inner'), slab_moves())  9.67 us
    pallas_call x1, Pallas kernels, correlate(): pl.pallas_call(kernel, out_shape=jax.ShapeDtypeStruct((rows, n_units), F3...  5.77 us
  transfers between devices with their start and end apart: 33, of which 18 were waited for; matrix products, arithmetic and copies ran while one was open for 1% of the time, Pallas kernels for 8%

profile of v1, /device:TPU:1, one launch (start us, length us, event | category | flops | bytes accessed | tf_op | source)
XLA Modules:
  0.0 207.3 jit_solution(14476332905119068478)
XLA Ops:
  0.0 0.7 copy-done.1
  0.7 2.3 %shard_map.66 = bf16[2,1024,896]{2,1,0:T(8,128)(2,1)S(1)} custom-call(s32[1]{0:T(128)S(1)} %bitcast.51, bf16[1024,1792]{1,0:T(8,128)(2,1)} %refs_0_.3, bf16[1024,1792]{1,0:T(8,128)(2,1)} %refs_1_.3), custom_call_target="tpu_custom_call" | custom-call | bytes 7340032 | tf_op jit(solution)/shard_map/pallas_call | solution.py:141
  2.9 1.5 collective-permute-start.18
  4.4 7.6 %shard_map.64 = (f32[2,224,1024]{2,1,0:T(8,128)S(1)}, bf16[2,224,1024]{2,1,0:T(8,128)(2,1)S(1)}, bf16[2,224,1024]{2,1,0:T(8,128)(2,1)S(1)}, bf16[2,224,1024]{2,1,0:T(8,128)(2,1)S(1)}) custom-call(bf16[1024,1792]{1,0:T(8,128)(2,1)} %w_ref.2, bf16[1024,1024]{1,0:T(8,128)(2,1)S(1)} %copy-done), custom_call_target="tpu_custom_call" | custom-call | flops 3758096384 | bytes 5767168 | tf_op jit(solution)/shard_map/pallas_call | solution.py:77
  12.0 3.1 %collective-permute-start = (bf16[2,224,1024]{2,1,0:T(8,128)(2,1)S(1)}, bf16[2,224,1024]{2,1,0:T(8,128)(2,1)S(1)}, u32[]{:S(2)}, u32[]{:S(2)}) collective-permute-start(bf16[2,224,1024]{2,1,0:T(8,128)(2,1)S(1)} %get-tuple-element.31), channel_id=1, source_target_pairs={{0,32},{16,48},{32,0},{48,16},{64,96},{80,112},{96,64},{112,80},{1... | collective-permute-start | bytes 2752520 | tf_op jit(solution)/shard_map/ppermute | solution.py:32
  15.1 7.6 %shard_map.65 = (f32[4,224,1024]{2,1,0:T(8,128)S(1)}, bf16[224,1024]{1,0:T(8,128)(2,1)S(1)}, bf16[224,1024]{1,0:T(8,128)(2,1)S(1)}, bf16[224,1024]{1,0:T(8,128)(2,1)S(1)}, bf16[224,1024]{1,0:T(8,128)(2,1)S(1)}) custom-call(bf16[1024,1792]{1,0:T(8,128)(2,1)} %w_ref.3, bf16[1024,1024]{1,0:T(8,128)(2,1)S(1)} %copy-done), custom_call_target="tpu_custom_call" | custom-call | flops 3758096384 | bytes 5767168 | tf_op jit(solution)/shard_map/pallas_call | solution.py:77
  22.8 1.7 collective-permute-start.4
  24.6 1.4 collective-permute-start.6
  25.9 8.7 %collective-permute-done.4 = bf16[224,1024]{1,0:T(8,128)(2,1)S(1)} collective-permute-done((bf16[224,1024]{1,0:T(8,128)(2,1)S(1)}, bf16[224,1024]{1,0:T(8,128)(2,1)S(1)}, u32[]{:S(2)}, u32[]{:S(2)}) %collective-permute-start.4) | collective-permute-done | bytes 458784 | tf_op jit(solution)/shard_map/ppermute | solution.py:32
  35.0 2.3 %collective-permute-start.2 = (bf16[2,224,1024]{2,1,0:T(8,128)(2,1)S(1)}, bf16[2,224,1024]{2,1,0:T(8,128)(2,1)S(1)}, u32[]{:S(2)}, u32[]{:S(2)}) collective-permute-start(bf16[2,224,1024]{2,1,0:T(8,128)(2,1)S(1)} %get-tuple-element.33), channel_id=1, source_target_pairs={{0,48},{16,0},{32,16},{48,32},{64,112},{80,64},{96,80},{112,96},{1... | collective-permute-start | bytes 2752520 | tf_op jit(solution)/shard_map/ppermute | solution.py:32
  37.9 6.6 %collective-permute-done.5 = bf16[224,1024]{1,0:T(8,128)(2,1)S(1)} collective-permute-done((bf16[224,1024]{1,0:T(8,128)(2,1)S(1)}, bf16[224,1024]{1,0:T(8,128)(2,1)S(1)}, u32[]{:S(2)}, u32[]{:S(2)}) %collective-permute-start.5) | collective-permute-done | bytes 458784 | tf_op jit(solution)/shard_map/ppermute | solution.py:32
  44.5 1.2 collective-permute-start.19
  45.7 8.6 %collective-permute-done.6 = bf16[224,1024]{1,0:T(8,128)(2,1)S(1)} collective-permute-done((bf16[224,1024]{1,0:T(8,128)(2,1)S(1)}, bf16[224,1024]{1,0:T(8,128)(2,1)S(1)}, u32[]{:S(2)}, u32[]{:S(2)}) %collective-permute-start.6) | collective-permute-done | bytes 458784 | tf_op jit(solution)/shard_map/ppermute | solution.py:32
  54.3 2.7 %collective-permute-start.20 = (bf16[2,1024,256]{2,1,0:T(8,128)(2,1)S(1)}, bf16[2,1024,256]{2,1,0:T(8,128)(2,1)S(1)}, u32[]{:S(2)}, u32[]{:S(2)}) collective-permute-start(bf16[2,1024,256]{2,1,0:T(8,128)(2,1)S(1)} %get-tuple-element.47), channel_id=1, source_target_pairs={{0,4},{1,5},{2,6},{3,7},{4,0},{5,1},{6,2},{7,3},{8,12},{9,13},{10,... | collective-permute-start | bytes 3145736 | tf_op jit(solution)/shard_map/ppermute | solution.py:36
  57.1 0.9 collective-permute-start.21
  58.1 1.4 collective-permute-start.7
  59.6 0.6 convert_add_fusion
  60.3 7.9 %collective-permute-done.19.refs_1_ = bf16[2,1024,256]{2,1,0:T(8,128)(2,1)S(1)} collective-permute-done((bf16[2,1024,256]{2,1,0:T(8,128)(2,1)S(1)}, bf16[2,1024,256]{2,1,0:T(8,128)(2,1)S(1)}, u32[]{:S(2)}, u32[]{:S(2)}) %collective-permute-start.19) | collective-permute-done | bytes 1048608 | tf_op jit(solution)/shard_map/ppermute | solution.py:36
  68.6 23.1 %collective-permute-done.20.refs_2_ = bf16[2,1024,256]{2,1,0:T(8,128)(2,1)S(1)} collective-permute-done((bf16[2,1024,256]{2,1,0:T(8,128)(2,1)S(1)}, bf16[2,1024,256]{2,1,0:T(8,128)(2,1)S(1)}, u32[]{:S(2)}, u32[]{:S(2)}) %collective-permute-start.20) | collective-permute-done | bytes 1048608 | tf_op jit(solution)/shard_map/ppermute | solution.py:36
  91.6 0.8 collective-permute-start.10
  92.4 10.0 %collective-permute-done.21.refs_3_ = bf16[2,1024,256]{2,1,0:T(8,128)(2,1)S(1)} collective-permute-done((bf16[2,1024,256]{2,1,0:T(8,128)(2,1)S(1)}, bf16[2,1024,256]{2,1,0:T(8,128)(2,1)S(1)}, u32[]{:S(2)}, u32[]{:S(2)}) %collective-permute-start.21) | collective-permute-done | bytes 1048608 | tf_op jit(solution)/shard_map/ppermute | solution.py:36
  102.4 1.3 collective-permute-start.3
  104.0 3.4 %collective-permute-start.22 = (bf16[2,1024,128]{2,1,0:T(8,128)(2,1)S(1)}, bf16[2,1024,128]{2,1,0:T(8,128)(2,1)S(1)}, u32[]{:S(2)}, u32[]{:S(2)}) collective-permute-start(bf16[2,1024,128]{2,1,0:T(8,128)(2,1)S(1)} %get-tuple-element.50), channel_id=1, source_target_pairs={{0,8},{1,9},{2,10},{3,11},{4,12},{5,13},{6,14},{7,15},{8,0},{9,1},... | collective-permute-start | bytes 1572872 | tf_op jit(solution)/shard_map/ppermute | solution.py:36
  107.4 5.5 %collective-permute-done.3 = bf16[224,1024]{1,0:T(8,128)(2,1)S(1)} collective-permute-done((bf16[224,1024]{1,0:T(8,128)(2,1)S(1)}, bf16[224,1024]{1,0:T(8,128)(2,1)S(1)}, u32[]{:S(2)}, u32[]{:S(2)}) %collective-permute-start.3) | collective-permute-done | bytes 458784 | tf_op jit(solution)/shard_map/ppermute | solution.py:32
  113.0 0.6 fusion.15
  113.8 13.5 %collective-permute-done.22.other_ref = bf16[2,1024,128]{2,1,0:T(8,128)(2,1)S(1)} collective-permute-done((bf16[2,1024,128]{2,1,0:T(8,128)(2,1)S(1)}, bf16[2,1024,128]{2,1,0:T(8,128)(2,1)S(1)}, u32[]{:S(2)}, u32[]{:S(2)}) %collective-permute-start.22) | collective-permute-done | bytes 524320 | tf_op jit(solution)/shard_map/ppermute | solution.py:36
  127.3 2.0 shard_map.69
  129.4 0.8 collective-permute-start.25
  130.2 1.4 collective-permute-start.24
  131.8 2.7 %collective-permute-start.16 = (bf16[224,1024]{1,0:T(8,128)(2,1)S(1)}, bf16[224,1024]{1,0:T(8,128)(2,1)S(1)}, u32[]{:S(2)}, u32[]{:S(2)}) collective-permute-start(bf16[224,1024]{1,0:T(8,128)(2,1)S(1)} %multiply_convert_fusion.refs_0_), channel_id=1, source_target_pairs={{0,48},{16,0},{32,16},{48,32},{64,112},{80,64},{96,80},{112,96},{1... | collective-permute-start | bytes 1376264 | tf_op jit(solution)/shard_map/ppermute | solution.py:32
  134.6 2.4 %collective-permute-done.24 = f32[2,2,16,1024]{3,2,0,1:T(8,128)S(1)} collective-permute-done((f32[2,2,16,1024]{3,2,0,1:T(8,128)S(1)}, f32[2,2,16,1024]{3,2,0,1:T(8,128)S(1)}, u32[]{:S(2)}, u32[]{:S(2)}) %collective-permute-start.24) | collective-permute-done | bytes 262176 | tf_op jit(solution)/shard_map/ppermute | solution.py:32
  137.0 7.6 %collective-permute-done.23 = f32[2,2,16,1024]{3,2,0,1:T(8,128)S(1)} collective-permute-done((f32[2,2,16,1024]{3,2,0,1:T(8,128)S(1)}, f32[2,2,16,1024]{3,2,0,1:T(8,128)S(1)}, u32[]{:S(2)}, u32[]{:S(2)}) %collective-permute-start.23) | collective-permute-done | bytes 262176 | tf_op jit(solution)/shard_map/ppermute | solution.py:32
  144.9 2.0 collective-permute-start.12
  146.9 1.3 collective-permute-start.11
  148.2 2.2 %collective-permute-done.16.refs_6_ = bf16[224,1024]{1,0:T(8,128)(2,1)S(1)} collective-permute-done((bf16[224,1024]{1,0:T(8,128)(2,1)S(1)}, bf16[224,1024]{1,0:T(8,128)(2,1)S(1)}, u32[]{:S(2)}, u32[]{:S(2)}) %collective-permute-start.16) | collective-permute-done | bytes 458784 | tf_op jit(solution)/shard_map/ppermute | solution.py:32
  150.8 9.7 %collective-permute-start.27 = (bf16[16,1024]{1,0:T(8,128)(2,1)S(1)}, bf16[16,1024]{1,0:T(8,128)(2,1)S(1)}, u32[]{:S(2)}, u32[]{:S(2)}) collective-permute-start(bf16[16,1024]{1,0:T(8,128)(2,1)S(1)} %multiply_convert_fusion.1), channel_id=1, source_target_pairs={{0,0},{16,1},{32,2},{48,3},{64,4},{80,5},{96,6},{112,7},{1,64},{17... | collective-permute-start | bytes 98312 | tf_op jit(solution)/shard_map/ppermute | solution.py:339
  160.5 1.8 collective-permute-start.15
  162.3 1.3 collective-permute-done.12.refs_2_
  163.6 1.1 collective-permute-start.13
  164.7 3.4 %collective-permute-done.27 = bf16[16,1024]{1,0:T(8,128)(2,1)S(1)} collective-permute-done((bf16[16,1024]{1,0:T(8,128)(2,1)S(1)}, bf16[16,1024]{1,0:T(8,128)(2,1)S(1)}, u32[]{:S(2)}, u32[]{:S(2)}) %collective-permute-start.27) | collective-permute-done | bytes 32800 | tf_op jit(solution)/shard_map/ppermute | solution.py:339
  168.1 2.8 %collective-permute-start.28 = (bf16[16,1024]{1,0:T(8,128)(2,1)S(1)}, bf16[16,1024]{1,0:T(8,128)(2,1)S(1)}, u32[]{:S(2)}, u32[]{:S(2)}) collective-permute-start(bf16[16,1024]{1,0:T(8,128)(2,1)S(1)} %collective-permute-done.27), channel_id=1, source_target_pairs={{0,1},{1,0},{2,3},{3,2},{4,5},{5,4},{6,7},{7,6},{8,9},{9,8},{10,11... | collective-permute-start | bytes 98312 | tf_op jit(solution)/shard_map/ppermute | solution.py:36
  170.9 0.9 collective-permute-done.28
  172.1 14.8 %collective-permute-done.29 = bf16[2,16,1024]{2,1,0:T(8,128)(2,1)S(1)} collective-permute-done((bf16[2,16,1024]{2,1,0:T(8,128)(2,1)S(1)}, bf16[2,16,1024]{2,1,0:T(8,128)(2,1)S(1)}, u32[]{:S(2)}, u32[]{:S(2)}) %collective-permute-start.29) | collective-permute-done | bytes 65568 | tf_op jit(solution)/shard_map/ppermute | solution.py:36
  187.0 8.0 %collective-permute-start.32 = (bf16[4,16,1024]{2,1,0:T(8,128)(2,1)S(1)}, bf16[4,16,1024]{2,1,0:T(8,128)(2,1)S(1)}, u32[]{:S(2)}, u32[]{:S(2)}) collective-permute-start(bf16[4,16,1024]{2,1,0:T(8,128)(2,1)S(1)} %pad_maximum_fusion.refs_8_), channel_id=1, source_target_pairs={{0,6},{1,7},{2,0},{3,1},{4,2},{5,3},{6,4},{7,5},{8,14},{9,15},{10,... | collective-permute-start | bytes 393224 | tf_op jit(solution)/shard_map/ppermute | solution.py:36
  195.0 1.3 collective-permute-start.30
  196.3 0.7 collective-permute-done.32.refs_11_
  196.9 4.5 %collective-permute-done.31.refs_10_ = bf16[4,16,1024]{2,1,0:T(8,128)(2,1)S(1)} collective-permute-done((bf16[4,16,1024]{2,1,0:T(8,128)(2,1)S(1)}, bf16[4,16,1024]{2,1,0:T(8,128)(2,1)S(1)}, u32[]{:S(2)}, u32[]{:S(2)}) %collective-permute-start.31) | collective-permute-done | bytes 131104 | tf_op jit(solution)/shard_map/ppermute | solution.py:36
  201.4 5.8 %shard_map.70 = f32[224,1792]{1,0:T(8,128)} custom-call(bf16[224,1024]{1,0:T(8,128)(2,1)S(1)} %multiply_convert_fusion.refs_0_, bf16[224,1024]{1,0:T(8,128)(2,1)S(1)} %collective-permute-done.11.refs_1_, bf16[224,1024]{1,0:T(8,128)(2,1)S(1)} %collective-permute-done.12.refs_2_, bf16[224,1024]{1,0:T(8,128)(2,1)S(1)} %collective-permute-done.13.refs_3_, ...), custom_call_target="tpu_custom_call" | custom-call | flops 822083584 | bytes 5734400 | tf_op jit(solution)/shard_map/pallas_call | solution.py:308
  (54 shorter events, 3.8 us)
Async XLA Ops:
  0.0 0.7 copy-start.1
  0.7 3.7 %copy-start = (bf16[1024,1024]{1,0:T(8,128)(2,1)S(1)}, bf16[1024,1024]{1,0:T(8,128)(2,1)}, u32[]{:S(2)}) copy-start(bf16[1024,1024]{1,0:T(8,128)(2,1)} %t_ref.5) | copy-start | bytes 6291460
  2.9 32.1 %collective-permute-start.18 = (bf16[2,1024,896]{2,1,0:T(8,128)(2,1)S(1)}, bf16[2,1024,896]{2,1,0:T(8,128)(2,1)S(1)}, u32[]{:S(2)}, u32[]{:S(2)}) collective-permute-start(bf16[2,1024,896]{2,1,0:T(8,128)(2,1)S(1)} %shard_map.66), channel_id=1, source_target_pairs={{0,1},{1,0},{2,3},{3,2},{4,5},{5,4},{6,7},{7,6},{8,9},{9,8},{10,11... | collective-permute-start | bytes 11010056 | tf_op jit(solution)/shard_map/ppermute | solution.py:36
  12.0 25.4 %copy-start.2 = (s32[16]{0:T(128)S(1)}, s32[16]{0:T(128)}, u32[]{:S(2)}) copy-start(s32[16]{0:T(128)} %param.11) | copy-start | bytes 196
  12.0 45.0 %collective-permute-start = (bf16[2,224,1024]{2,1,0:T(8,128)(2,1)S(1)}, bf16[2,224,1024]{2,1,0:T(8,128)(2,1)S(1)}, u32[]{:S(2)}, u32[]{:S(2)}) collective-permute-start(bf16[2,224,1024]{2,1,0:T(8,128)(2,1)S(1)} %get-tuple-element.31), channel_id=1, source_target_pairs={{0,32},{16,48},{32,0},{48,16},{64,96},{80,112},{96,64},{112,80},{1... | collective-permute-start | bytes 2752520 | tf_op jit(solution)/shard_map/ppermute | solution.py:32
  22.8 11.9 %collective-permute-start.4 = (bf16[224,1024]{1,0:T(8,128)(2,1)S(1)}, bf16[224,1024]{1,0:T(8,128)(2,1)S(1)}, u32[]{:S(2)}, u32[]{:S(2)}) collective-permute-start(bf16[224,1024]{1,0:T(8,128)(2,1)S(1)} %get-tuple-element.35), channel_id=1, source_target_pairs={{0,64},{16,80},{32,96},{48,112},{64,0},{80,16},{96,32},{112,48},{1... | collective-permute-start | bytes 1376264 | tf_op jit(solution)/shard_map/ppermute | solution.py:32
  24.5 20.0 %collective-permute-start.5 = (bf16[224,1024]{1,0:T(8,128)(2,1)S(1)}, bf16[224,1024]{1,0:T(8,128)(2,1)S(1)}, u32[]{:S(2)}, u32[]{:S(2)}) collective-permute-start(bf16[224,1024]{1,0:T(8,128)(2,1)S(1)} %get-tuple-element.37), channel_id=1, source_target_pairs={{0,64},{16,80},{32,96},{48,112},{64,0},{80,16},{96,32},{112,48},{1... | collective-permute-start | bytes 1376264 | tf_op jit(solution)/shard_map/ppermute | solution.py:32
  24.6 29.7 %collective-permute-start.6 = (bf16[224,1024]{1,0:T(8,128)(2,1)S(1)}, bf16[224,1024]{1,0:T(8,128)(2,1)S(1)}, u32[]{:S(2)}, u32[]{:S(2)}) collective-permute-start(bf16[224,1024]{1,0:T(8,128)(2,1)S(1)} %get-tuple-element.39), channel_id=1, source_target_pairs={{0,64},{16,80},{32,96},{48,112},{64,0},{80,16},{96,32},{112,48},{1... | collective-permute-start | bytes 1376264 | tf_op jit(solution)/shard_map/ppermute | solution.py:32
  34.6 23.5 %collective-permute-start.1 = (bf16[2,224,1024]{2,1,0:T(8,128)(2,1)S(1)}, bf16[2,224,1024]{2,1,0:T(8,128)(2,1)S(1)}, u32[]{:S(2)}, u32[]{:S(2)}) collective-permute-start(bf16[2,224,1024]{2,1,0:T(8,128)(2,1)S(1)} %get-tuple-element.32), channel_id=1, source_target_pairs={{0,16},{16,32},{32,48},{48,0},{64,80},{80,96},{96,112},{112,64},{1... | collective-permute-start | bytes 2752520 | tf_op jit(solution)/shard_map/ppermute | solution.py:32
  35.0 24.5 %collective-permute-start.2 = (bf16[2,224,1024]{2,1,0:T(8,128)(2,1)S(1)}, bf16[2,224,1024]{2,1,0:T(8,128)(2,1)S(1)}, u32[]{:S(2)}, u32[]{:S(2)}) collective-permute-start(bf16[2,224,1024]{2,1,0:T(8,128)(2,1)S(1)} %get-tuple-element.33), channel_id=1, source_target_pairs={{0,48},{16,0},{32,16},{48,32},{64,112},{80,64},{96,80},{112,96},{1... | collective-permute-start | bytes 2752520 | tf_op jit(solution)/shard_map/ppermute | solution.py:32
  44.5 23.7 %collective-permute-start.19 = (bf16[2,1024,256]{2,1,0:T(8,128)(2,1)S(1)}, bf16[2,1024,256]{2,1,0:T(8,128)(2,1)S(1)}, u32[]{:S(2)}, u32[]{:S(2)}) collective-permute-start(bf16[2,1024,256]{2,1,0:T(8,128)(2,1)S(1)} %get-tuple-element.46), channel_id=1, source_target_pairs={{0,2},{1,3},{2,4},{3,5},{4,6},{5,7},{6,0},{7,1},{8,10},{9,11},{10,... | collective-permute-start | bytes 3145736 | tf_op jit(solution)/shard_map/ppermute | solution.py:36
  54.3 37.3 %collective-permute-start.20 = (bf16[2,1024,256]{2,1,0:T(8,128)(2,1)S(1)}, bf16[2,1024,256]{2,1,0:T(8,128)(2,1)S(1)}, u32[]{:S(2)}, u32[]{:S(2)}) collective-permute-start(bf16[2,1024,256]{2,1,0:T(8,128)(2,1)S(1)} %get-tuple-element.47), channel_id=1, source_target_pairs={{0,4},{1,5},{2,6},{3,7},{4,0},{5,1},{6,2},{7,3},{8,12},{9,13},{10,... | collective-permute-start | bytes 3145736 | tf_op jit(solution)/shard_map/ppermute | solution.py:36
  57.1 45.4 %collective-permute-start.21 = (bf16[2,1024,256]{2,1,0:T(8,128)(2,1)S(1)}, bf16[2,1024,256]{2,1,0:T(8,128)(2,1)S(1)}, u32[]{:S(2)}, u32[]{:S(2)}) collective-permute-start(bf16[2,1024,256]{2,1,0:T(8,128)(2,1)S(1)} %get-tuple-element.48), channel_id=1, source_target_pairs={{0,6},{1,7},{2,0},{3,1},{4,2},{5,3},{6,4},{7,5},{8,14},{9,15},{10,... | collective-permute-start | bytes 3145736 | tf_op jit(solution)/shard_map/ppermute | solution.py:36
  58.1 45.9 %collective-permute-start.7 = (bf16[224,1024]{1,0:T(8,128)(2,1)S(1)}, bf16[224,1024]{1,0:T(8,128)(2,1)S(1)}, u32[]{:S(2)}, u32[]{:S(2)}) collective-permute-start(bf16[224,1024]{1,0:T(8,128)(2,1)S(1)} %get-tuple-element.41), channel_id=1, source_target_pairs={{0,64},{16,80},{32,96},{48,112},{64,0},{80,16},{96,32},{112,48},{1... | collective-permute-start | bytes 1376264 | tf_op jit(solution)/shard_map/ppermute | solution.py:32
  59.5 47.9 %collective-permute-start.8 = (bf16[224,1024]{1,0:T(8,128)(2,1)S(1)}, bf16[224,1024]{1,0:T(8,128)(2,1)S(1)}, u32[]{:S(2)}, u32[]{:S(2)}) collective-permute-start(bf16[224,1024]{1,0:T(8,128)(2,1)S(1)} %fusion.7), channel_id=1, source_target_pairs={{0,32},{16,48},{32,0},{48,16},{64,96},{80,112},{96,64},{112,80},{1... | collective-permute-start | bytes 1376264 | tf_op jit(solution)/shard_map/ppermute | solution.py:32
  68.2 39.2 %collective-permute-start.9 = (bf16[224,1024]{1,0:T(8,128)(2,1)S(1)}, bf16[224,1024]{1,0:T(8,128)(2,1)S(1)}, u32[]{:S(2)}, u32[]{:S(2)}) collective-permute-start(bf16[224,1024]{1,0:T(8,128)(2,1)S(1)} %fusion.6), channel_id=1, source_target_pairs={{0,16},{16,32},{32,48},{48,0},{64,80},{80,96},{96,112},{112,64},{1... | collective-permute-start | bytes 1376264 | tf_op jit(solution)/shard_map/ppermute | solution.py:32
  91.6 15.8 %collective-permute-start.10 = (bf16[224,1024]{1,0:T(8,128)(2,1)S(1)}, bf16[224,1024]{1,0:T(8,128)(2,1)S(1)}, u32[]{:S(2)}, u32[]{:S(2)}) collective-permute-start(bf16[224,1024]{1,0:T(8,128)(2,1)S(1)} %fusion.5), channel_id=1, source_target_pairs={{0,48},{16,0},{32,16},{48,32},{64,112},{80,64},{96,80},{112,96},{1... | collective-permute-start | bytes 1376264 | tf_op jit(solution)/shard_map/ppermute | solution.py:32
  102.4 10.5 %collective-permute-start.3 = (bf16[224,1024]{1,0:T(8,128)(2,1)S(1)}, bf16[224,1024]{1,0:T(8,128)(2,1)S(1)}, u32[]{:S(2)}, u32[]{:S(2)}) collective-permute-start(bf16[224,1024]{1,0:T(8,128)(2,1)S(1)} %fusion.8), channel_id=1, source_target_pairs={{0,64},{16,80},{32,96},{48,112},{64,0},{80,16},{96,32},{112,48},{1... | collective-permute-start | bytes 1376264 | tf_op jit(solution)/shard_map/ppermute | solution.py:32
  104.0 23.3 %collective-permute-start.22 = (bf16[2,1024,128]{2,1,0:T(8,128)(2,1)S(1)}, bf16[2,1024,128]{2,1,0:T(8,128)(2,1)S(1)}, u32[]{:S(2)}, u32[]{:S(2)}) collective-permute-start(bf16[2,1024,128]{2,1,0:T(8,128)(2,1)S(1)} %get-tuple-element.50), channel_id=1, source_target_pairs={{0,8},{1,9},{2,10},{3,11},{4,12},{5,13},{6,14},{7,15},{8,0},{9,1},... | collective-permute-start | bytes 1572872 | tf_op jit(solution)/shard_map/ppermute | solution.py:36
  129.4 5.3 %collective-permute-start.25 = (f32[2,2,16,1024]{3,2,0,1:T(8,128)S(1)}, f32[2,2,16,1024]{3,2,0,1:T(8,128)S(1)}, u32[]{:S(2)}, u32[]{:S(2)}) collective-permute-start(f32[2,2,16,1024]{3,2,0,1:T(8,128)S(1)} %copy.10), channel_id=1, source_target_pairs={{0,48},{16,0},{32,16},{48,32},{64,112},{80,64},{96,80},{112,96},{1... | collective-permute-start | bytes 786440 | tf_op jit(solution)/shard_map/ppermute | solution.py:32
  130.2 6.8 %collective-permute-start.24 = (f32[2,2,16,1024]{3,2,0,1:T(8,128)S(1)}, f32[2,2,16,1024]{3,2,0,1:T(8,128)S(1)}, u32[]{:S(2)}, u32[]{:S(2)}) collective-permute-start(f32[2,2,16,1024]{3,2,0,1:T(8,128)S(1)} %copy.9), channel_id=1, source_target_pairs={{0,32},{16,48},{32,0},{48,16},{64,96},{80,112},{96,64},{112,80},{1... | collective-permute-start | bytes 786440 | tf_op jit(solution)/shard_map/ppermute | solution.py:32
  131.6 13.0 %collective-permute-start.23 = (f32[2,2,16,1024]{3,2,0,1:T(8,128)S(1)}, f32[2,2,16,1024]{3,2,0,1:T(8,128)S(1)}, u32[]{:S(2)}, u32[]{:S(2)}) collective-permute-start(f32[2,2,16,1024]{3,2,0,1:T(8,128)S(1)} %copy.7), channel_id=1, source_target_pairs={{0,16},{16,32},{32,48},{48,0},{64,80},{80,96},{96,112},{112,64},{1... | collective-permute-start | bytes 786440 | tf_op jit(solution)/shard_map/ppermute | solution.py:32
  131.8 18.5 %collective-permute-start.16 = (bf16[224,1024]{1,0:T(8,128)(2,1)S(1)}, bf16[224,1024]{1,0:T(8,128)(2,1)S(1)}, u32[]{:S(2)}, u32[]{:S(2)}) collective-permute-start(bf16[224,1024]{1,0:T(8,128)(2,1)S(1)} %multiply_convert_fusion.refs_0_), channel_id=1, source_target_pairs={{0,48},{16,0},{32,16},{48,32},{64,112},{80,64},{96,80},{112,96},{1... | collective-permute-start | bytes 1376264 | tf_op jit(solution)/shard_map/ppermute | solution.py:32
  144.7 5.6 %collective-permute-start.26 = (f32[2,16,1024]{2,1,0:T(8,128)S(1)}, f32[2,16,1024]{2,1,0:T(8,128)S(1)}, u32[]{:S(2)}, u32[]{:S(2)}) collective-permute-start(f32[2,16,1024]{2,1,0:T(8,128)S(1)} %slice_bitcast_fusion.1), channel_id=1, source_target_pairs={{0,64},{16,80},{32,96},{48,112},{64,0},{80,16},{96,32},{112,48},{1... | collective-permute-start | bytes 393224 | tf_op jit(solution)/shard_map/ppermute | solution.py:32
  144.8 15.7 %collective-permute-start.14 = (bf16[224,1024]{1,0:T(8,128)(2,1)S(1)}, bf16[224,1024]{1,0:T(8,128)(2,1)S(1)}, u32[]{:S(2)}, u32[]{:S(2)}) collective-permute-start(bf16[224,1024]{1,0:T(8,128)(2,1)S(1)} %multiply_convert_fusion.refs_0_), channel_id=1, source_target_pairs={{0,16},{16,32},{32,48},{48,0},{64,80},{80,96},{96,112},{112,64},{1... | collective-permute-start | bytes 1376264 | tf_op jit(solution)/shard_map/ppermute | solution.py:32
  144.9 18.7 %collective-permute-start.12 = (bf16[224,1024]{1,0:T(8,128)(2,1)S(1)}, bf16[224,1024]{1,0:T(8,128)(2,1)S(1)}, u32[]{:S(2)}, u32[]{:S(2)}) collective-permute-start(bf16[224,1024]{1,0:T(8,128)(2,1)S(1)} %multiply_convert_fusion.refs_0_), channel_id=1, source_target_pairs={{0,32},{16,48},{32,0},{48,16},{64,96},{80,112},{96,64},{112,80},{1... | collective-permute-start | bytes 1376264 | tf_op jit(solution)/shard_map/ppermute | solution.py:32
  146.9 48.1 %collective-permute-start.11 = (bf16[224,1024]{1,0:T(8,128)(2,1)S(1)}, bf16[224,1024]{1,0:T(8,128)(2,1)S(1)}, u32[]{:S(2)}, u32[]{:S(2)}) collective-permute-start(bf16[224,1024]{1,0:T(8,128)(2,1)S(1)} %multiply_convert_fusion.refs_0_), channel_id=1, source_target_pairs={{0,64},{16,80},{32,96},{48,112},{64,0},{80,16},{96,32},{112,48},{1... | collective-permute-start | bytes 1376264 | tf_op jit(solution)/shard_map/ppermute | solution.py:32
  150.3 44.7 %collective-permute-start.17 = (bf16[224,1024]{1,0:T(8,128)(2,1)S(1)}, bf16[224,1024]{1,0:T(8,128)(2,1)S(1)}, u32[]{:S(2)}, u32[]{:S(2)}) collective-permute-start(bf16[224,1024]{1,0:T(8,128)(2,1)S(1)} %collective-permute-done.16.refs_6_), channel_id=1, source_target_pairs={{0,64},{16,80},{32,96},{48,112},{64,0},{80,16},{96,32},{112,48},{1... | collective-permute-start | bytes 1376264 | tf_op jit(solution)/shard_map/ppermute | solution.py:32
  150.8 17.3 %collective-permute-start.27 = (bf16[16,1024]{1,0:T(8,128)(2,1)S(1)}, bf16[16,1024]{1,0:T(8,128)(2,1)S(1)}, u32[]{:S(2)}, u32[]{:S(2)}) collective-permute-start(bf16[16,1024]{1,0:T(8,128)(2,1)S(1)} %multiply_convert_fusion.1), channel_id=1, source_target_pairs={{0,0},{16,1},{32,2},{48,3},{64,4},{80,5},{96,6},{112,7},{1,64},{17... | collective-permute-start | bytes 98312 | tf_op jit(solution)/shard_map/ppermute | solution.py:339
  160.5 35.8 %collective-permute-start.15 = (bf16[224,1024]{1,0:T(8,128)(2,1)S(1)}, bf16[224,1024]{1,0:T(8,128)(2,1)S(1)}, u32[]{:S(2)}, u32[]{:S(2)}) collective-permute-start(bf16[224,1024]{1,0:T(8,128)(2,1)S(1)} %collective-permute-done.14.refs_4_), channel_id=1, source_target_pairs={{0,64},{16,80},{32,96},{48,112},{64,0},{80,16},{96,32},{112,48},{1... | collective-permute-start | bytes 1376264 | tf_op jit(solution)/shard_map/ppermute | solution.py:32
  163.6 32.7 %collective-permute-start.13 = (bf16[224,1024]{1,0:T(8,128)(2,1)S(1)}, bf16[224,1024]{1,0:T(8,128)(2,1)S(1)}, u32[]{:S(2)}, u32[]{:S(2)}) collective-permute-start(bf16[224,1024]{1,0:T(8,128)(2,1)S(1)} %collective-permute-done.12.refs_2_), channel_id=1, source_target_pairs={{0,64},{16,80},{32,96},{48,112},{64,0},{80,16},{96,32},{112,48},{1... | collective-permute-start | bytes 1376264 | tf_op jit(solution)/shard_map/ppermute | solution.py:32
  168.1 3.6 %collective-permute-start.28 = (bf16[16,1024]{1,0:T(8,128)(2,1)S(1)}, bf16[16,1024]{1,0:T(8,128)(2,1)S(1)}, u32[]{:S(2)}, u32[]{:S(2)}) collective-permute-start(bf16[16,1024]{1,0:T(8,128)(2,1)S(1)} %collective-permute-done.27), channel_id=1, source_target_pairs={{0,1},{1,0},{2,3},{3,2},{4,5},{5,4},{6,7},{7,6},{8,9},{9,8},{10,11... | collective-permute-start | bytes 98312 | tf_op jit(solution)/shard_map/ppermute | solution.py:36
  171.7 15.2 %collective-permute-start.29 = (bf16[2,16,1024]{2,1,0:T(8,128)(2,1)S(1)}, bf16[2,16,1024]{2,1,0:T(8,128)(2,1)S(1)}, u32[]{:S(2)}, u32[]{:S(2)}) collective-permute-start(bf16[2,16,1024]{2,1,0:T(8,128)(2,1)S(1)} %pad_maximum_fusion.1), channel_id=1, source_target_pairs={{0,8},{1,9},{2,10},{3,11},{4,12},{5,13},{6,14},{7,15},{8,0},{9,1},... | collective-permute-start | bytes 196616 | tf_op jit(solution)/shard_map/ppermute | solution.py:36
  187.0 9.9 %collective-permute-start.32 = (bf16[4,16,1024]{2,1,0:T(8,128)(2,1)S(1)}, bf16[4,16,1024]{2,1,0:T(8,128)(2,1)S(1)}, u32[]{:S(2)}, u32[]{:S(2)}) collective-permute-start(bf16[4,16,1024]{2,1,0:T(8,128)(2,1)S(1)} %pad_maximum_fusion.refs_8_), channel_id=1, source_target_pairs={{0,6},{1,7},{2,0},{3,1},{4,2},{5,3},{6,4},{7,5},{8,14},{9,15},{10,... | collective-permute-start | bytes 393224 | tf_op jit(solution)/shard_map/ppermute | solution.py:36
  195.0 6.4 %collective-permute-start.31 = (bf16[4,16,1024]{2,1,0:T(8,128)(2,1)S(1)}, bf16[4,16,1024]{2,1,0:T(8,128)(2,1)S(1)}, u32[]{:S(2)}, u32[]{:S(2)}) collective-permute-start(bf16[4,16,1024]{2,1,0:T(8,128)(2,1)S(1)} %pad_maximum_fusion.refs_8_), channel_id=1, source_target_pairs={{0,2},{1,3},{2,4},{3,5},{4,6},{5,7},{6,0},{7,1},{8,10},{9,11},{10,... | collective-permute-start | bytes 393224 | tf_op jit(solution)/shard_map/ppermute | solution.py:36
  195.0 6.4 %collective-permute-start.30 = (bf16[4,16,1024]{2,1,0:T(8,128)(2,1)S(1)}, bf16[4,16,1024]{2,1,0:T(8,128)(2,1)S(1)}, u32[]{:S(2)}, u32[]{:S(2)}) collective-permute-start(bf16[4,16,1024]{2,1,0:T(8,128)(2,1)S(1)} %pad_maximum_fusion.refs_8_), channel_id=1, source_target_pairs={{0,4},{1,5},{2,6},{3,7},{4,0},{5,1},{6,2},{7,3},{8,12},{9,13},{10,... | collective-permute-start | bytes 393224 | tf_op jit(solution)/shard_map/ppermute | solution.py:36
